TPU v7x, 32 devices: a whole 2x2x4 slice. The times are simulated.
32 devices in a mesh: seq: 8 (over y, x, core), tp: 4 (over z).
Axes of the slice: x: 2, y: 2, z: 4, core: 2. Of those that a mesh axis runs over, the one named last changes fastest.
Arguments:
- stream: bfloat16 [16384, 1024], P(('seq', 'tp')), may hold values from -6 to 6
- segments: int32 [16384], replicated, may hold values from 0 to 63, never falling along the last dimension, each value on 1 to 1024 neighbouring positions
- skip_values: bfloat16 [16384, 512], P('seq', 'tp'), may hold values from -6 to 6
- first_gain: float32 [1024], replicated, may hold values from 0.5 to 1.5
- first_shift: float32 [1024], replicated, may hold values from -1.75 to 1.75
- query_weight: bfloat16 [1024, 1024], P(None, 'tp'), may hold values from -0.1875 to 0.1875
- query_bias: float32 [1024], P('tp'), may hold values from -3 to 3
- key_weight: bfloat16 [1024, 1024], P(None, 'tp'), may hold values from -0.1875 to 0.1875
- value_weight: bfloat16 [1024, 512], P(None, 'tp'), may hold values from -0.1875 to 0.1875
- value_bias: float32 [512], P('tp'), may hold values from -3 to 3
- mixing_weight: bfloat16 [1024, 1024], P('tp'), may hold values from -1.5 to 1.5
- mixing_bias: float32 [1024], replicated, may hold values from -1.75 to 1.75
- second_gain: float32 [1024], replicated, may hold values from 0.5 to 1.5
- second_shift: float32 [1024], replicated, may hold values from -1.75 to 1.75
- up_weight: bfloat16 [1024, 4096], P(None, 'tp'), may hold values from -0.1875 to 0.1875
- up_bias: float32 [4096], P('tp'), may hold values from -3 to 3
- down_weight: bfloat16 [4096, 1024], P('tp'), may hold values from -0.09375 to 0.09375
- down_bias: float32 [1024], replicated, may hold values from -1.75 to 1.75
- cotangent: bfloat16 [16384, 1024], P(('seq', 'tp')), may hold values from -6 to 6
Outputs:
- output: bfloat16 [16384, 1024], P(('seq', 'tp'))
- stream_gradient: float32 [16384, 1024], P(('seq', 'tp'))
- skip_gradient: float32 [16384, 512], P('seq', 'tp')
- query_gradient: float32 [1024, 1024], P('seq', 'tp')
- query_bias_gradient: float32 [1024], replicated
- key_gradient: float32 [1024, 1024], P('seq', 'tp')
- value_gradient: float32 [1024, 512], P('seq', 'tp')
- value_bias_gradient: float32 [512], replicated
- mixing_gradient: float32 [1024, 1024], P('tp', 'seq')
- mixing_bias_gradient: float32 [1024], replicated
- first_gain_gradient: float32 [1024], replicated
- first_shift_gradient: float32 [1024], replicated
- second_gain_gradient: float32 [1024], replicated
- second_shift_gradient: float32 [1024], replicated
- up_gradient: float32 [1024, 4096], P('seq', 'tp')
- up_bias_gradient: float32 [4096], replicated
- down_gradient: float32 [4096, 1024], P('tp', 'seq')
- down_bias_gradient: float32 [1024], replicated
Inputs may be any that keep to these rules, and one draw needn't show every extreme that they name: `segments`: segment numbers never fall along the stream; each document spans 1 to 1024 tokens, and some document spans exactly 1024.
All inputs are finite; a program needn't handle non-finite values.
Results may differ from a plain program's by a relative error of at most 0.012.
Values may be sent and summed in bfloat16 or wider, within the bound.
No kernel may reach another device: no remote copies, remote signals or barrier semaphores. Data moves between devices by JAX's collectives and lax.ppermute only.
A program may use at most 128 MiB of HBM per device.

v0:
```python
import jax
import jax.numpy as jnp
from jax import lax
from jax.sharding import PartitionSpec as P

HEAD = 64
QUERY_BLOCK = 512
DOC_MAX = 1024
epsilon = 1e-05


def shifted(value, axis, steps):
    count = lax.axis_size(axis)
    leading, last = (max(0, -steps), min(count, count - steps))
    return lax.ppermute(value, axis, [(source, source + steps) for source in range(leading, last)])


def layer_norm(matrix, scale_gain, scale_shift):
    average = jnp.mean(matrix, axis=-1, keepdims=True)
    centered = matrix - average
    inverse = lax.rsqrt(jnp.mean(centered * centered, axis=-1, keepdims=True) + epsilon)
    return centered * inverse * scale_gain + scale_shift


def gelu_tanh(hidden):
    return jax.nn.gelu(hidden, approximate=True)


def merge_values(fresh, reused):
    row_count = fresh.shape[0]
    groups = fresh.shape[1] // (2 * HEAD)
    paired = jnp.stack(
        (fresh.reshape(row_count, groups, 2 * HEAD), reused.reshape(row_count, groups, 2 * HEAD)),
        axis=2,
    )
    return paired.reshape(row_count, 4 * groups * HEAD)


def split_values(merged):
    row_count = merged.shape[0]
    groups = merged.shape[1] // (4 * HEAD)
    paired = merged.reshape(row_count, groups, 2, 2 * HEAD)
    return (
        paired[:, :, 0].reshape(row_count, groups * 2 * HEAD),
        paired[:, :, 1].reshape(row_count, groups * 2 * HEAD),
    )


def rows_product(first_operand, second_operand):
    return lax.dot_general(
        first_operand, second_operand, (((0,), (0,)), ((), ())), preferred_element_type=jnp.float32
    )


def transposed_product(first_operand, second_operand):
    return lax.dot_general(
        first_operand, second_operand, (((1,), (1,)), ((), ())), preferred_element_type=jnp.float32
    )


def masked_scores(query_block, key_window, segment_query, segment_key):
    row_count = query_block.shape[0]
    window = key_window.shape[0]
    heads = query_block.shape[1] // HEAD
    scores = jnp.einsum(
        "qhd,khd->hqk",
        query_block.reshape(row_count, heads, HEAD),
        key_window.reshape(window, heads, HEAD),
        preferred_element_type=jnp.float32,
    ) * HEAD ** (-0.5)
    allowed = (segment_query[:, None] == segment_key[None, :]) & (
        jnp.arange(window)[None, :] <= jnp.arange(row_count)[:, None] + DOC_MAX
    )
    return jnp.where(allowed[None], scores, -1e30)


def widen(partial_sum, full_length, place):
    return lax.dynamic_update_slice_in_dim(
        jnp.zeros((full_length,), jnp.float32), partial_sum, place * partial_sum.shape[0], 0
    )


def local(
    stream,
    segments,
    skip_values,
    first_gain,
    first_shift,
    query_weight,
    query_bias,
    key_weight,
    value_weight,
    value_bias,
    mixing_weight,
    mixing_bias,
    second_gain,
    second_shift,
    up_weight,
    up_bias,
    down_weight,
    down_bias,
    cotangent,
):
    width = query_weight.shape[1]
    tok_count = skip_values.shape[0]
    block_count = tok_count // QUERY_BLOCK
    window = DOC_MAX + QUERY_BLOCK
    heads = width // HEAD
    tp_count = lax.axis_size("tp")
    seq_place = lax.axis_index("seq")
    tp_place = lax.axis_index("tp")
    stream_wide = stream.astype(jnp.float32)
    first_normed, first_pullback = jax.vjp(layer_norm, stream_wide, first_gain, first_shift)
    gathered_first = lax.all_gather(first_normed.astype(jnp.bfloat16), "tp", axis=0, tiled=True)
    query = (
        jnp.dot(gathered_first, query_weight, preferred_element_type=jnp.float32) + query_bias
    ).astype(jnp.bfloat16)
    keys = jnp.dot(gathered_first, key_weight, preferred_element_type=jnp.float32).astype(
        jnp.bfloat16
    )
    fresh = (
        jnp.dot(gathered_first, value_weight, preferred_element_type=jnp.float32) + value_bias
    ).astype(jnp.bfloat16)
    values = merge_values(fresh, skip_values)
    earlier = shifted(
        jnp.stack((keys[tok_count - DOC_MAX :], values[tok_count - DOC_MAX :])), "seq", 1
    )
    keys_ext = jnp.concatenate((earlier[0], keys), axis=0)
    values_ext = jnp.concatenate((earlier[1], values), axis=0)
    segment_padded = jnp.concatenate((jnp.full((DOC_MAX,), -1, jnp.int32), segments))
    segment_ext = lax.dynamic_slice_in_dim(
        segment_padded, seq_place * tok_count, DOC_MAX + tok_count, 0
    )

    def forward_block(block_index):
        row_start = block_index * QUERY_BLOCK
        query_block = lax.dynamic_slice_in_dim(query, row_start, QUERY_BLOCK, 0)
        key_window = lax.dynamic_slice_in_dim(keys_ext, row_start, window, 0)
        value_window = lax.dynamic_slice_in_dim(values_ext, row_start, window, 0)
        scores = masked_scores(
            query_block,
            key_window,
            lax.dynamic_slice_in_dim(segment_ext, row_start + DOC_MAX, QUERY_BLOCK, 0),
            lax.dynamic_slice_in_dim(segment_ext, row_start, window, 0),
        )
        maximum = jnp.max(scores, axis=-1, keepdims=True)
        exponent = jnp.exp(scores - maximum)
        denominator = jnp.sum(exponent, axis=-1, keepdims=True)
        probability = (exponent / denominator).astype(jnp.bfloat16)
        mixed = jnp.einsum(
            "hqk,khd->qhd",
            probability,
            value_window.reshape(window, heads, HEAD),
            preferred_element_type=jnp.float32,
        )
        return (
            mixed.reshape(QUERY_BLOCK, width).astype(jnp.bfloat16),
            maximum[..., 0] + jnp.log(denominator[..., 0]),
        )

    attended_blocks, log_totals = lax.map(forward_block, jnp.arange(block_count, dtype=jnp.int32))
    attended = attended_blocks.reshape(tok_count, width)
    middle = (
        stream_wide
        + lax.psum_scatter(
            jnp.dot(attended, mixing_weight, preferred_element_type=jnp.float32),
            "tp",
            scatter_dimension=0,
            tiled=True,
        )
        + mixing_bias
    )
    second_normed, second_pullback = jax.vjp(layer_norm, middle, second_gain, second_shift)
    gathered_second = lax.all_gather(second_normed.astype(jnp.bfloat16), "tp", axis=0, tiled=True)
    hidden = jnp.dot(gathered_second, up_weight, preferred_element_type=jnp.float32) + up_bias
    activated_wide, gelu_pullback = jax.vjp(gelu_tanh, hidden)
    activated = activated_wide.astype(jnp.bfloat16)
    output = (
        middle
        + lax.psum_scatter(
            jnp.dot(activated, down_weight, preferred_element_type=jnp.float32).astype(
                jnp.bfloat16
            ),
            "tp",
            scatter_dimension=0,
            tiled=True,
        ).astype(jnp.float32)
        + down_bias
    ).astype(jnp.bfloat16)
    upstream = cotangent.astype(jnp.float32)
    cotangent_all = lax.all_gather(cotangent, "tp", axis=0, tiled=True)
    activated_back = transposed_product(cotangent_all, down_weight)
    down_local = rows_product(activated, cotangent_all)
    hidden_back = gelu_pullback(activated_back)[0].astype(jnp.bfloat16)
    unit_column = jnp.ones((tok_count,), jnp.bfloat16)
    up_bias_part = jnp.dot(unit_column, hidden_back, preferred_element_type=jnp.float32)
    up_local = rows_product(gathered_second, hidden_back)
    second_normed_back = lax.psum_scatter(
        transposed_product(hidden_back, up_weight), "tp", scatter_dimension=0, tiled=True
    )
    middle_from_norm, second_gain_part, second_shift_part = second_pullback(second_normed_back)
    middle_back = upstream + middle_from_norm
    middle_all = lax.all_gather(middle_back.astype(jnp.bfloat16), "tp", axis=0, tiled=True)
    attended_back = transposed_product(middle_all, mixing_weight).astype(jnp.bfloat16)
    mixing_local = rows_product(attended, middle_all)

    def backward_block(carried, block_index):
        key_sum, value_sum = carried
        row_start = block_index * QUERY_BLOCK
        query_block = lax.dynamic_slice_in_dim(query, row_start, QUERY_BLOCK, 0)
        key_window = lax.dynamic_slice_in_dim(keys_ext, row_start, window, 0)
        value_window = lax.dynamic_slice_in_dim(values_ext, row_start, window, 0)
        scores = masked_scores(
            query_block,
            key_window,
            lax.dynamic_slice_in_dim(segment_ext, row_start + DOC_MAX, QUERY_BLOCK, 0),
            lax.dynamic_slice_in_dim(segment_ext, row_start, window, 0),
        )
        probability = jnp.exp(scores - log_totals[block_index][..., None])
        out_back = lax.dynamic_slice_in_dim(attended_back, row_start, QUERY_BLOCK, 0).reshape(
            QUERY_BLOCK, heads, HEAD
        )
        prob_back = jnp.einsum(
            "qhd,khd->hqk",
            out_back,
            value_window.reshape(window, heads, HEAD),
            preferred_element_type=jnp.float32,
        )
        correction = jnp.sum(probability * prob_back, axis=-1, keepdims=True)
        score_back = (probability * (prob_back - correction)).astype(jnp.bfloat16)
        query_part = jnp.einsum(
            "hqk,khd->qhd",
            score_back,
            key_window.reshape(window, heads, HEAD),
            preferred_element_type=jnp.float32,
        ) * HEAD ** (-0.5)
        key_part = jnp.einsum(
            "hqk,qhd->khd",
            score_back,
            query_block.reshape(QUERY_BLOCK, heads, HEAD),
            preferred_element_type=jnp.float32,
        ) * HEAD ** (-0.5)
        value_part = jnp.einsum(
            "hqk,qhd->khd",
            probability.astype(jnp.bfloat16),
            out_back,
            preferred_element_type=jnp.float32,
        )
        key_sum = lax.dynamic_update_slice_in_dim(
            key_sum,
            lax.dynamic_slice_in_dim(key_sum, row_start, window, 0)
            + key_part.reshape(window, width),
            row_start,
            0,
        )
        value_sum = lax.dynamic_update_slice_in_dim(
            value_sum,
            lax.dynamic_slice_in_dim(value_sum, row_start, window, 0)
            + value_part.reshape(window, width),
            row_start,
            0,
        )
        return ((key_sum, value_sum), query_part.reshape(QUERY_BLOCK, width))

    empty_sum = jnp.zeros((DOC_MAX + tok_count, width), jnp.float32)
    (key_ext_back, value_ext_back), query_blocks = lax.scan(
        backward_block, (empty_sum, empty_sum), jnp.arange(block_count, dtype=jnp.int32)
    )
    returned = shifted(
        jnp.stack((key_ext_back[:DOC_MAX], value_ext_back[:DOC_MAX])).astype(jnp.bfloat16),
        "seq",
        -1,
    ).astype(jnp.float32)
    key_back = jnp.concatenate(
        (key_ext_back[DOC_MAX:tok_count], key_ext_back[tok_count:] + returned[0]), axis=0
    ).astype(jnp.bfloat16)
    value_back = jnp.concatenate(
        (value_ext_back[DOC_MAX:tok_count], value_ext_back[tok_count:] + returned[1]), axis=0
    )
    fresh_wide, skip_gradient = split_values(value_back)
    fresh_back = fresh_wide.astype(jnp.bfloat16)
    query_back = query_blocks.reshape(tok_count, width).astype(jnp.bfloat16)
    query_bias_part = jnp.dot(unit_column, query_back, preferred_element_type=jnp.float32)
    value_bias_part = jnp.dot(unit_column, fresh_back, preferred_element_type=jnp.float32)
    query_local = rows_product(gathered_first, query_back)
    key_local = rows_product(gathered_first, key_back)
    value_local = rows_product(gathered_first, fresh_back)
    total = transposed_product(query_back, query_weight)
    total = total + transposed_product(key_back, key_weight)
    first_normed_back = lax.psum_scatter(
        total + transposed_product(fresh_back, value_weight), "tp", scatter_dimension=0, tiled=True
    )
    stream_from_norm, first_gain_part, first_shift_part = first_pullback(first_normed_back)
    stream_gradient = middle_back + stream_from_norm
    (
        first_gain_gradient,
        first_shift_gradient,
        second_gain_gradient,
        second_shift_gradient,
        mixing_bias_gradient,
        down_bias_gradient,
        query_bias_gradient,
        value_bias_gradient,
        up_bias_gradient,
    ) = lax.psum(
        (
            first_gain_part,
            first_shift_part,
            second_gain_part,
            second_shift_part,
            jnp.sum(middle_back, axis=0),
            jnp.sum(upstream, axis=0),
            widen(query_bias_part, width * tp_count, tp_place),
            widen(value_bias_part, value_bias_part.shape[0] * tp_count, tp_place),
            widen(up_bias_part, up_bias_part.shape[0] * tp_count, tp_place),
        ),
        ("seq", "tp"),
    )
    query_gradient, key_gradient, value_gradient, mixing_gradient, up_gradient, down_gradient = (
        lax.psum_scatter(query_local, "seq", scatter_dimension=0, tiled=True),
        lax.psum_scatter(key_local, "seq", scatter_dimension=0, tiled=True),
        lax.psum_scatter(value_local, "seq", scatter_dimension=0, tiled=True),
        lax.psum_scatter(mixing_local, "seq", scatter_dimension=1, tiled=True),
        lax.psum_scatter(up_local, "seq", scatter_dimension=0, tiled=True),
        lax.psum_scatter(down_local, "seq", scatter_dimension=1, tiled=True),
    )
    return (
        output,
        stream_gradient,
        skip_gradient,
        query_gradient,
        query_bias_gradient,
        key_gradient,
        value_gradient,
        value_bias_gradient,
        mixing_gradient,
        mixing_bias_gradient,
        first_gain_gradient,
        first_shift_gradient,
        second_gain_gradient,
        second_shift_gradient,
        up_gradient,
        up_bias_gradient,
        down_gradient,
        down_bias_gradient,
    )


def solution(mesh):
    in_specs = (
        P(("seq", "tp"), None),
        P(),
        P("seq", "tp"),
        P(),
        P(),
        P(None, "tp"),
        P("tp"),
        P(None, "tp"),
        P(None, "tp"),
        P("tp"),
        P("tp", None),
        P(),
        P(),
        P(),
        P(None, "tp"),
        P("tp"),
        P("tp", None),
        P(),
        P(("seq", "tp"), None),
    )
    out_specs = (
        P(("seq", "tp"), None),
        P(("seq", "tp"), None),
        P("seq", "tp"),
        P("seq", "tp"),
        P(),
        P("seq", "tp"),
        P("seq", "tp"),
        P(),
        P("tp", "seq"),
        P(),
        P(),
        P(),
        P(),
        P(),
        P("seq", "tp"),
        P(),
        P("tp", "seq"),
        P(),
    )
    return jax.shard_map(local, mesh=mesh, in_specs=in_specs, out_specs=out_specs, check_vma=False)
```

profile of v0, /device:TPU:0, one launch (start us, length us, event | category | flops | bytes accessed | tf_op | source)
XLA Modules:
  0.0 1425.8 jit_solution(13958946887283911155)
XLA Ops:
  13.6 83.3 %all-gather.5.cloned.1.call-done = bf16[2048,1024]{1,0:T(8,128)(2,1)} async-done(((bf16[512,1024]{1,0:T(8,128)(2,1)}), bf16[2048,1024]{1,0:T(8,128)(2,1)}) %all-gather.5.cloned.1.call-update) | async-done | bytes 4194320 | tf_op jit(solution)/shard_map/all_gather | solution.py:114
  96.9 3.7 fusion.25
  103.5 3.6 convolution_convert_fusion.2
  112.0 4.5 fusion.21
  130.2 64.8 %while.30 = (s32[]{:T(128)}, bf16[4,512,256]{2,1,0:T(8,128)(2,1)}, f32[4,4,512]{2,1,0:T(4,128)S(1)}, s32[4]{0:T(128)S(1)}, bf16[3072,256]{0,1:T(8,128)(2,1)}, /*...) while((s32[]{:T(128)}, bf16[4,512,256]{2,1,0:T(8,128)(2,1)}, ...), condition=%wide.region_5.6_spmd, body=%wide.region_2.5_spmd.sunk | while | flops 845543936 | bytes 47804716 | solution.py:161
  141.0 4.5 fusion.144
  157.2 4.5 fusion.144
  173.4 4.5 fusion.144
  189.6 4.5 fusion.144
  195.0 5.7 fusion.67
  200.8 148.9 %reduce-scatter.11.cloned.1.call-done = f32[512,1024]{1,0:T(8,128)} async-done(((f32[2048,1024]{1,0:T(8,128)}), f32[512,1024]{1,0:T(8,128)}) %reduce-scatter.11.cloned.1.call-update) | async-done | bytes 2097168 | tf_op jit(solution)/shard_map/reduce_scatter | solution.py:165
  355.3 80.6 %all-gather.7.cloned.1.call-done = bf16[2048,1024]{1,0:T(8,128)(2,1)} async-done(((bf16[512,1024]{1,0:T(8,128)(2,1)}), bf16[2048,1024]{1,0:T(8,128)(2,1)}) %all-gather.7.cloned.1.call-update) | async-done | bytes 4194320 | tf_op jit(solution)/shard_map/all_gather | solution.py:174
  435.9 8.9 fusion.68
  444.8 71.8 %all-gather.9.cloned.1.call-done = bf16[2048,1024]{1,0:T(8,128)(2,1)} async-done(((bf16[512,1024]{1,0:T(8,128)(2,1)}), bf16[2048,1024]{1,0:T(8,128)(2,1)}) %all-gather.9.cloned.1.call-update) | async-done | bytes 4194320 | tf_op jit(solution)/shard_map/all_gather | solution.py:191
  516.6 12.7 fusion.16
  531.3 7.0 fusion.69
  539.8 11.4 convolution_convert_fusion
  551.4 130.2 %reduce-scatter.15.cloned.1.call-done = f32[512,1024]{1,0:T(8,128)} async-done(((f32[2048,1024]{1,0:T(8,128)}), f32[512,1024]{1,0:T(8,128)}) %reduce-scatter.15.cloned.1.call-update) | async-done | bytes 2097168 | tf_op jit(solution)/shard_map/reduce_scatter | solution.py:198
  684.5 76.6 %reduce-scatter.13.cloned.1.call-done = bf16[512,1024]{1,0:T(8,128)(2,1)} async-done(((bf16[2048,1024]{1,0:T(8,128)(2,1)}), bf16[512,1024]{1,0:T(8,128)(2,1)}) %reduce-scatter.13.cloned.1.call-update) | async-done | bytes 1048592 | tf_op jit(solution)/shard_map/reduce_scatter | solution.py:180
  761.1 3.7 fusion.61
  767.5 81.4 %all-gather.11.cloned.1.call-done = bf16[2048,1024]{1,0:T(8,128)(2,1)} async-done(((bf16[512,1024]{1,0:T(8,128)(2,1)}), bf16[2048,1024]{1,0:T(8,128)(2,1)}) %all-gather.11.cloned.1.call-update) | async-done | bytes 4194320 | tf_op jit(solution)/shard_map/all_gather | solution.py:203
  848.8 4.5 convolution_convert_fusion.1
  857.4 122.1 %while.31 = (s32[]{:T(128)}, f32[3072,256]{0,1:T(8,128)}, f32[3072,256]{0,1:T(8,128)}, bf16[4,512,256]{2,1,0:T(8,128)(2,1)}, s32[4]{0:T(128)S(1)}, /*index=5*/bf...) while((s32[]{:T(128)}, f32[3072,256]{0,1:T(8,128)}, ...), condition=%wide.region_15.16_spmd, body=%wide.region_13.15_spmd.sunk | while | flops 2045377024 | bytes 155783632 | solution.py:266
  867.1 4.3 multiply_reduce_fusion.5
  871.4 3.6 multiply_convert_fusion.5
  884.1 4.0 constant_dynamic-update-slice_fusion.8
  897.6 4.3 multiply_reduce_fusion.5
  901.9 3.6 multiply_convert_fusion.5
  914.6 4.0 constant_dynamic-update-slice_fusion.8
  928.1 4.3 multiply_reduce_fusion.5
  945.0 4.0 constant_dynamic-update-slice_fusion.8
  958.6 4.3 multiply_reduce_fusion.5
  975.6 4.0 constant_dynamic-update-slice_fusion.8
  992.3 4.6 add_add_fusion
  997.0 10.0 fusion.73
  1007.7 12.6 fusion.59
  1020.4 4.9 fusion.72
  1025.3 4.4 fusion.71
  1033.3 4.4 fusion.52
  1038.1 4.5 fusion.35
  1046.7 104.6 %reduce-scatter.17.cloned.1.call-done = f32[512,1024]{1,0:T(8,128)} async-done(((f32[2048,1024]{1,0:T(8,128)}), f32[512,1024]{1,0:T(8,128)}) %reduce-scatter.17.cloned.1.call-update) | async-done | bytes 2097168 | tf_op jit(solution)/shard_map/reduce_scatter | solution.py:290
  1157.0 42.2 %all-reduce.1 = (f32[1024]{0:T(1024)}, f32[512]{0:T(512)}, f32[1024]{0:T(1024)}, f32[1024]{0:T(1024)}, f32[1024]{0:T(1024)}, /*index=5*/f32[1024]{0:T(1024)}, f32[1024]{0:T(1024)}, f32[4096]{0:T(1024)}, f32[1024]{0:T(1024)}) all-reduce(f32[1024]{0:T(1024)S(1)} %dynamic_update_slice.42, ...), channel_id=1, replica_groups=mesh['seq'=8,'tp'=4] {'seq','tp'}, use_global_device_ids=true, to_apply=%region_20.21 | all-reduce | flops 11776 | bytes 94208 | tf_op jit(solution)/shard_map/psum | solution.py:305
  1199.2 8.0 reduce-scatter.27.cloned.1.call-done
  1207.2 54.9 %reduce-scatter.29.cloned.1.call-done = f32[1024,128]{1,0:T(8,128)} async-done(((f32[1024,1024]{1,0:T(8,128)}), f32[1024,128]{1,0:T(8,128)}) %reduce-scatter.29.cloned.1.call-update) | async-done | bytes 524304 | tf_op jit(solution)/shard_map/reduce_scatter | solution.py:325
  1262.0 39.7 %reduce-scatter.25.cloned.1.call-done = f32[256,128]{1,0:T(8,128)} async-done(((f32[256,1024]{1,0:T(8,128)}), f32[256,128]{1,0:T(8,128)}) %reduce-scatter.25.cloned.1.call-update) | async-done | bytes 131088 | tf_op jit(solution)/shard_map/reduce_scatter | solution.py:323
  1301.8 39.6 %reduce-scatter.19.cloned.1.call-done = f32[128,256]{1,0:T(8,128)} async-done(((f32[1024,256]{1,0:T(8,128)}), f32[128,256]{1,0:T(8,128)}) %reduce-scatter.19.cloned.1.call-update) | async-done | bytes 131088 | tf_op jit(solution)/shard_map/reduce_scatter | solution.py:320
  1341.4 37.8 %reduce-scatter.23.cloned.1.call-done = f32[128,128]{1,0:T(8,128)} async-done(((f32[1024,128]{1,0:T(8,128)}), f32[128,128]{1,0:T(8,128)}) %reduce-scatter.23.cloned.1.call-update) | async-done | bytes 65552 | tf_op jit(solution)/shard_map/reduce_scatter | solution.py:322
  1379.2 39.6 %reduce-scatter.21.cloned.1.call-done = f32[128,256]{1,0:T(8,128)} async-done(((f32[1024,256]{1,0:T(8,128)}), f32[128,256]{1,0:T(8,128)}) %reduce-scatter.21.cloned.1.call-update) | async-done | bytes 131088 | tf_op jit(solution)/shard_map/reduce_scatter | solution.py:321
  (333 shorter events, 188.3 us)
Async XLA Ops:
  7.2 428.7 %copy-start = (bf16[1024,1024]{1,0:T(8,128)(2,1)S(1)}, bf16[1024,1024]{1,0:T(8,128)(2,1)}, u32[]{:S(2)}) copy-start(bf16[1024,1024]{1,0:T(8,128)(2,1)} %param.37) | copy-start | bytes 6291460
  7.2 6.1 copy-start.31
  7.2 89.7 %copy-start.25 = (bf16[1024,128]{1,0:T(8,128)(2,1)S(1)}, bf16[1024,128]{1,0:T(8,128)(2,1)}, u32[]{:S(2)}) copy-start(bf16[1024,128]{1,0:T(8,128)(2,1)} %param.31) | copy-start | bytes 786436
  7.2 89.6 %copy-start.48 = (f32[128]{0:T(128)S(1)}, f32[128]{0:T(128)}, u32[]{:S(2)}) copy-start(f32[128]{0:T(128)} %param.32) | copy-start | bytes 1540
  7.2 89.6 %all-gather.5.cloned.1.call-start = ((), (), s32[]{:S(2)}) async-start(), calls=%async_computation.10 | async-start | bytes 5242880 | tf_op jit(solution)/shard_map/all_gather | solution.py:114
  8.9 4.4 copy-start.32
  13.3 336.4 %reduce-scatter.11.cloned.1.call-start = ((), (), s32[]{:S(2)}) async-start(), calls=%async_computation.11 | async-start | bytes 10485760 | tf_op jit(solution)/shard_map/reduce_scatter | solution.py:165
  103.5 4.7 copy-start.22
  108.1 3.9 copy-start.35
  108.1 4.0 copy-start.52
  109.2 10.7 collective-permute-start
  122.0 5.9 copy-start.16
  130.2 64.8 %copy-start.27 = (bf16[256,1024]{1,0:T(8,128)(2,1)S(1)}, bf16[256,1024]{1,0:T(8,128)(2,1)}, u32[]{:S(2)}) copy-start(bf16[256,1024]{1,0:T(8,128)(2,1)} %param.33) | copy-start | bytes 1572868
  200.7 149.0 %copy-start.8 = (bf16[512,1024]{1,0:T(8,128)(2,1)S(1)}, bf16[512,1024]{1,0:T(8,128)(2,1)}, u32[]{:S(2)}) copy-start(bf16[512,1024]{1,0:T(8,128)(2,1)} %param.23) | copy-start | bytes 3145732
  200.7 149.0 %copy-start.47 = (f32[1024]{0:T(1024)S(1)}, f32[1024]{0:T(1024)}, u32[]{:S(2)}) copy-start(f32[1024]{0:T(1024)} %param.34) | copy-start | bytes 12292
  200.8 152.2 %copy-start.36 = (f32[1024]{0:T(1024)S(1)}, f32[1024]{0:T(1024)}, u32[]{:S(2)}) copy-start(f32[1024]{0:T(1024)} %param.35) | copy-start | bytes 12292
  200.8 152.2 %copy-start.45 = (f32[1024]{0:T(1024)S(1)}, f32[1024]{0:T(1024)}, u32[]{:S(2)}) copy-start(f32[1024]{0:T(1024)} %param.36) | copy-start | bytes 12292
  200.8 235.1 %all-gather.7.cloned.1.call-start = ((), (), s32[]{:S(2)}) async-start(), calls=%async_computation.12 | async-start | bytes 5242880 | tf_op jit(solution)/shard_map/all_gather | solution.py:174
  354.4 162.2 %all-gather.9.cloned.1.call-start = ((), (), s32[]{:S(2)}) async-start(), calls=%async_computation.14 | async-start | bytes 5242880 | tf_op jit(solution)/shard_map/all_gather | solution.py:191
  355.0 161.6 %copy-start.50 = (f32[1024]{0:T(1024)S(1)}, f32[1024]{0:T(1024)}, u32[]{:S(2)}) copy-start(f32[1024]{0:T(1024)} %param.38) | copy-start | bytes 12292
  355.0 326.6 %reduce-scatter.15.cloned.1.call-start = ((), (), s32[]{:S(2)}) async-start(), calls=%async_computation.15 | async-start | bytes 10485760 | tf_op jit(solution)/shard_map/reduce_scatter | solution.py:198
  538.3 222.8 %reduce-scatter.13.cloned.1.call-start = ((), (), s32[]{:S(2)}) async-start(), calls=%async_computation.13 | async-start | bytes 5242880 | tf_op jit(solution)/shard_map/reduce_scatter | solution.py:180
  551.3 130.2 %copy-start.7 = (f32[512,1024]{1,0:T(8,128)S(1)}, f32[512,1024]{1,0:T(8,128)}, u32[]{:S(2)}) copy-start(f32[512,1024]{1,0:T(8,128)} %copy-done.6) | copy-start | bytes 6291460
  551.3 209.8 %copy-start.46 = (f32[1024]{0:T(1024)S(1)}, f32[1024]{0:T(1024)}, u32[]{:S(2)}) copy-start(f32[1024]{0:T(1024)} %param.40) | copy-start | bytes 12292
  551.3 297.5 %all-gather.11.cloned.1.call-start = ((), (), s32[]{:S(2)}) async-start(), calls=%async_computation.16 | async-start | bytes 5242880 | tf_op jit(solution)/shard_map/all_gather | solution.py:203
  684.5 81.6 %copy-start.13 = (bf16[512,1024]{1,0:T(8,128)(2,1)S(1)}, bf16[512,1024]{1,0:T(8,128)(2,1)}, u32[]{:S(2)}) copy-start(bf16[512,1024]{1,0:T(8,128)(2,1)} %param.41) | copy-start | bytes 3145732
  764.8 84.0 %copy-start.28 = (bf16[256,1024]{1,0:T(8,128)(2,1)S(1)}, bf16[256,1024]{1,0:T(8,128)(2,1)}, u32[]{:S(2)}) copy-start(bf16[256,1024]{1,0:T(8,128)(2,1)} %param.33) | copy-start | bytes 1572868
  764.8 88.6 %copy-start.39 = (f32[512]{0:T(512)}, f32[512]{0:T(512)S(1)}, u32[]{:S(2)}) copy-start(f32[512]{0:T(512)S(1)} %negate_multiply_fusion.1) | copy-start | bytes 6148
  767.4 383.9 %reduce-scatter.17.cloned.1.call-start = ((), (), s32[]{:S(2)}) async-start(), calls=%async_computation.17 | async-start | bytes 10485760 | tf_op jit(solution)/shard_map/reduce_scatter | solution.py:290
  983.0 9.2 copy-start.20
  983.2 4.7 collective-permute-start.1
  996.9 210.2 %reduce-scatter.27.cloned.1.call-start = ((), (), s32[]{:S(2)}) async-start(), calls=%async_computation.22 | async-start | bytes 4718592 | tf_op jit(solution)/shard_map/reduce_scatter | solution.py:324
  1007.0 255.0 %reduce-scatter.29.cloned.1.call-start = ((), (), s32[]{:S(2)}) async-start(), calls=%async_computation.23 | async-start | bytes 4718592 | tf_op jit(solution)/shard_map/reduce_scatter | solution.py:325
  1020.3 281.5 %reduce-scatter.25.cloned.1.call-start = ((), (), s32[]{:S(2)}) async-start(), calls=%async_computation.21 | async-start | bytes 1179648 | tf_op jit(solution)/shard_map/reduce_scatter | solution.py:323
  1025.3 316.1 %reduce-scatter.19.cloned.1.call-start = ((), (), s32[]{:S(2)}) async-start(), calls=%async_computation.18 | async-start | bytes 1179648 | tf_op jit(solution)/shard_map/reduce_scatter | solution.py:320
  1029.8 349.4 %reduce-scatter.23.cloned.1.call-start = ((), (), s32[]{:S(2)}) async-start(), calls=%async_computation.20 | async-start | bytes 589824 | tf_op jit(solution)/shard_map/reduce_scatter | solution.py:322
  1033.3 4.8 copy-start.21
  1033.3 4.8 copy-start.24
  1037.8 381.0 %reduce-scatter.21.cloned.1.call-start = ((), (), s32[]{:S(2)}) async-start(), calls=%async_computation.19 | async-start | bytes 1179648 | tf_op jit(solution)/shard_map/reduce_scatter | solution.py:321
  1042.6 108.7 %copy-start.9 = (bf16[512,1024]{1,0:T(8,128)(2,1)S(1)}, bf16[512,1024]{1,0:T(8,128)(2,1)}, u32[]{:S(2)}) copy-start(bf16[512,1024]{1,0:T(8,128)(2,1)} %param.23) | copy-start | bytes 3145732
  1042.6 108.7 %copy-start.33 = (f32[512]{0:T(512)S(1)}, f32[512]{0:T(512)}, u32[]{:S(2)}) copy-start(f32[512]{0:T(512)} %copy-done.32) | copy-start | bytes 6148
  1042.6 108.7 %copy-start.34 = (f32[1024]{0:T(1024)S(1)}, f32[1024]{0:T(1024)}, u32[]{:S(2)}) copy-start(f32[1024]{0:T(1024)} %param.26) | copy-start | bytes 12292
  1043.7 109.9 %copy-start.42 = (f32[512]{0:T(512)S(1)}, f32[512]{0:T(512)}, u32[]{:S(2)}) copy-start(f32[512]{0:T(512)} %copy-done.41) | copy-start | bytes 6148
  1043.7 109.9 %copy-start.38 = (f32[512]{0:T(512)S(1)}, f32[512]{0:T(512)}, u32[]{:S(2)}) copy-start(f32[512]{0:T(512)} %copy-done.37) | copy-start | bytes 6148
  1046.7 108.0 %copy-start.40 = (f32[512]{0:T(512)S(1)}, f32[512]{0:T(512)}, u32[]{:S(2)}) copy-start(f32[512]{0:T(512)} %copy-done.39) | copy-start | bytes 6148
  1151.3 3.4 copy-start.12
  1151.3 3.4 copy-start.14
  1154.6 264.1 %copy-start.1 = (bf16[1024,1024]{1,0:T(8,128)(2,1)S(1)}, bf16[1024,1024]{1,0:T(8,128)(2,1)}, u32[]{:S(2)}) copy-start(bf16[1024,1024]{1,0:T(8,128)(2,1)} %param.37) | copy-start | bytes 6291460
  (30 other events, 72.2 us)
Sparse Core Ops, SparseCore 0:
  13.4 83.4 all-gather.4
  200.9 148.7 reduce-scatter.10
  354.5 81.3 all-gather.6
  437.3 79.2 all-gather.8
  538.4 143.0 reduce-scatter.14
  683.7 77.3 reduce-scatter.12
  767.5 81.2 all-gather.10
  997.0 154.1 reduce-scatter.16
  1155.2 51.9 reduce-scatter.26
  1210.9 51.0 reduce-scatter.28
  1265.8 35.9 reduce-scatter.24
  1305.4 35.9 reduce-scatter.18
  1345.0 34.0 reduce-scatter.22
  1382.8 35.9 reduce-scatter.20
where the time goes:
time: 1430 us
  waiting for transfers between devices  999 us (70%)
  matrix products  191 us (13%)
  other arithmetic  85.1 us (6%)
  local copies, waits for them, and re-layouts  72.8 us (5%)
  blocking collectives  42.2 us (3%)
  between operations  15.1 us (1%)
    reduce_scatter x1, waiting for transfers between devices, local(): lax.psum_scatter(jnp.dot(attended, mixing_weight, preferred_element_type=...  149 us
    reduce_scatter x1, waiting for transfers between devices, local(): lax.psum_scatter(transposed_product(hidden_back, up_weight), 'tp', scatte...  130 us
    reduce_scatter x1, waiting for transfers between devices, local(): lax.psum_scatter(total + transposed_product(fresh_back, value_weight), 't...  105 us
    all_gather x1, waiting for transfers between devices, local(): lax.all_gather(first_normed.astype(jnp.bfloat16), 'tp', axis=0, tiled=True)  83.3 us
    all_gather x1, waiting for transfers between devices, local(): lax.all_gather(middle_back.astype(jnp.bfloat16), 'tp', axis=0, tiled=True)  81.4 us
    all_gather x1, waiting for transfers between devices, local(): lax.all_gather(second_normed.astype(jnp.bfloat16), 'tp', axis=0, tiled=True)  80.6 us
    reduce_scatter x1, waiting for transfers between devices, local(): lax.psum_scatter(jnp.dot(activated, down_weight, preferred_element_type=j...  76.6 us
    all_gather x1, waiting for transfers between devices, local(): cotangent_all = lax.all_gather(cotangent, 'tp', axis=0, tiled=True)  71.8 us
  transfers between devices with their start and end apart: 16, of which 15 were waited for; matrix products, arithmetic and copies ran while one was open for 6% of the time, Pallas kernels for 0%

commit v1 on v0

--- a/solution.py
+++ b/solution.py
@@ -200,7 +200,15 @@
     )
     middle_from_norm, second_gain_part, second_shift_part = second_pullback(second_normed_back)
     middle_back = upstream + middle_from_norm
-    middle_all = lax.all_gather(middle_back.astype(jnp.bfloat16), "tp", axis=0, tiled=True)
+    value_2 = middle_back.astype(jnp.bfloat16)
+    ways = lax.axis_size("tp")
+    pieces = [value_2]
+    for far in range(1, ways):
+        pieces.append(
+            lax.ppermute(pieces[far - 1], "tp", [(d, (d - 1) % ways) for d in range(ways)])
+        )
+    line = jnp.concatenate(pieces, axis=0)
+    middle_all = jnp.roll(line, lax.axis_index("tp") * value_2.shape[0], axis=0)
     attended_back = transposed_product(middle_all, mixing_weight).astype(jnp.bfloat16)
     mixing_local = rows_product(attended, middle_all)
 

time: 1430 us -> 1440 us (level)
  waiting for transfers between devices: 999 us -> 981 us
    all_gather x1 -> x0, waiting for transfers between devices: 81.4 us -> none  [local(): lax.all_gather(middle_back.astype(jnp.bfloat16), 'tp', axis=0, tiled=True)]
    ppermute x0 -> x3, waiting for transfers between devices: none -> 63 us  [local(): lax.ppermute(pieces[far - 1], 'tp', [(d, (d - 1) % ways) for d in range(w...]
  transfers between devices with their start and end apart: 16 -> 18, of which waited for: 15 -> 17; matrix products, arithmetic and copies ran while one was open for 6% -> 6% of each run, Pallas kernels for 0% -> 0%
where the time goes in v1:
time: 1440 us; the launch traced here: 1430 us
  waiting for transfers between devices  981 us (68%)
  matrix products  191 us (13%)
  other arithmetic  86.9 us (6%)
  local copies, waits for them, and re-layouts  86 us (6%)
  blocking collectives  42.2 us (3%)
  starting transfers between devices  17.2 us (1%)
  between operations  15 us (1%)
    reduce_scatter x1, waiting for transfers between devices, local(): lax.psum_scatter(jnp.dot(attended, mixing_weight, preferred_element_type=...  149 us
    reduce_scatter x1, waiting for transfers between devices, local(): lax.psum_scatter(transposed_product(hidden_back, up_weight), 'tp', scatte...  130 us
    reduce_scatter x1, waiting for transfers between devices, local(): lax.psum_scatter(total + transposed_product(fresh_back, value_weight), 't...  106 us
    all_gather x1, waiting for transfers between devices, local(): lax.all_gather(first_normed.astype(jnp.bfloat16), 'tp', axis=0, tiled=True)  83.3 us
    all_gather x1, waiting for transfers between devices, local(): lax.all_gather(second_normed.astype(jnp.bfloat16), 'tp', axis=0, tiled=True)  80.6 us
    reduce_scatter x1, waiting for transfers between devices, local(): lax.psum_scatter(jnp.dot(activated, down_weight, preferred_element_type=j...  76.7 us
    all_gather x1, waiting for transfers between devices, local(): cotangent_all = lax.all_gather(cotangent, 'tp', axis=0, tiled=True)  71.8 us
    ppermute x3, waiting for transfers between devices, local(): lax.ppermute(pieces[far - 1], 'tp', [(d, (d - 1) % ways) for d in range(w...  63 us
  transfers between devices with their start and end apart: 18, of which 17 were waited for; matrix products, arithmetic and copies ran while one was open for 6% of the time, Pallas kernels for 0%

profile of v1, /device:TPU:0, one launch (start us, length us, event | category | flops | bytes accessed | tf_op | source)
XLA Modules:
  0.0 1433.7 jit_solution(12079551122018002318)
XLA Ops:
  13.6 83.3 %all-gather.4.cloned.1.call-done = bf16[2048,1024]{1,0:T(8,128)(2,1)} async-done(((bf16[512,1024]{1,0:T(8,128)(2,1)}), bf16[2048,1024]{1,0:T(8,128)(2,1)}) %all-gather.4.cloned.1.call-update) | async-done | bytes 4194320 | tf_op jit(solution)/shard_map/all_gather | solution.py:114
  112.1 4.5 fusion.28
  130.3 64.8 %while.30 = (s32[]{:T(128)}, bf16[4,512,256]{2,1,0:T(8,128)(2,1)}, f32[4,4,512]{2,1,0:T(4,128)S(1)}, s32[4]{0:T(128)S(1)}, bf16[3072,256]{0,1:T(8,128)(2,1)}, /*...) while((s32[]{:T(128)}, bf16[4,512,256]{2,1,0:T(8,128)(2,1)}, ...), condition=%wide.region_5.6_spmd, body=%wide.region_2.5_spmd.sunk | while | flops 845543936 | bytes 47804716 | solution.py:161
  141.0 4.5 fusion.151
  157.2 4.5 fusion.151
  173.4 4.5 fusion.151
  189.6 4.5 fusion.151
  195.0 5.8 fusion.77
  200.9 148.8 %reduce-scatter.11.cloned.1.call-done = f32[512,1024]{1,0:T(8,128)} async-done(((f32[2048,1024]{1,0:T(8,128)}), f32[512,1024]{1,0:T(8,128)}) %reduce-scatter.11.cloned.1.call-update) | async-done | bytes 2097168 | tf_op jit(solution)/shard_map/reduce_scatter | solution.py:165
  355.3 80.6 %all-gather.6.cloned.1.call-done = bf16[2048,1024]{1,0:T(8,128)(2,1)} async-done(((bf16[512,1024]{1,0:T(8,128)(2,1)}), bf16[2048,1024]{1,0:T(8,128)(2,1)}) %all-gather.6.cloned.1.call-update) | async-done | bytes 4194320 | tf_op jit(solution)/shard_map/all_gather | solution.py:174
  435.9 8.9 fusion.78
  444.8 71.8 %all-gather.8.cloned.1.call-done = bf16[2048,1024]{1,0:T(8,128)(2,1)} async-done(((bf16[512,1024]{1,0:T(8,128)(2,1)}), bf16[2048,1024]{1,0:T(8,128)(2,1)}) %all-gather.8.cloned.1.call-update) | async-done | bytes 4194320 | tf_op jit(solution)/shard_map/all_gather | solution.py:191
  516.6 12.7 fusion.16
  531.3 6.9 fusion.79
  539.8 11.4 convolution_convert_fusion
  551.4 130.2 %reduce-scatter.15.cloned.1.call-done = f32[512,1024]{1,0:T(8,128)} async-done(((f32[2048,1024]{1,0:T(8,128)}), f32[512,1024]{1,0:T(8,128)}) %reduce-scatter.15.cloned.1.call-update) | async-done | bytes 2097168 | tf_op jit(solution)/shard_map/reduce_scatter | solution.py:198
  684.5 76.7 %reduce-scatter.13.cloned.1.call-done = bf16[512,1024]{1,0:T(8,128)(2,1)} async-done(((bf16[2048,1024]{1,0:T(8,128)(2,1)}), bf16[512,1024]{1,0:T(8,128)(2,1)}) %reduce-scatter.13.cloned.1.call-update) | async-done | bytes 1048592 | tf_op jit(solution)/shard_map/reduce_scatter | solution.py:180
  770.0 22.6 %collective-permute-done.1 = bf16[512,1024]{1,0:T(8,128)(2,1)S(1)} collective-permute-done((bf16[512,1024]{1,0:T(8,128)(2,1)S(1)}, bf16[512,1024]{1,0:T(8,128)(2,1)S(1)}, u32[]{:S(2)}, u32[]{:S(2)}) %collective-permute-start.1) | collective-permute-done | bytes 1048608 | tf_op jit(solution)/shard_map/ppermute | solution.py:208
  792.6 4.3 collective-permute-start.2
  796.9 21.7 %collective-permute-done.2 = bf16[512,1024]{1,0:T(8,128)(2,1)S(1)} collective-permute-done((bf16[512,1024]{1,0:T(8,128)(2,1)S(1)}, bf16[512,1024]{1,0:T(8,128)(2,1)S(1)}, u32[]{:S(2)}, u32[]{:S(2)}) %collective-permute-start.2) | collective-permute-done | bytes 1048608 | tf_op jit(solution)/shard_map/ppermute | solution.py:208
  818.6 4.3 collective-permute-start.3
  825.0 18.7 %collective-permute-done.3 = bf16[512,1024]{1,0:T(8,128)(2,1)} collective-permute-done((bf16[512,1024]{1,0:T(8,128)(2,1)S(1)}, bf16[512,1024]{1,0:T(8,128)(2,1)}, u32[]{:S(2)}, u32[]{:S(2)}) %collective-permute-start.3) | collective-permute-done | bytes 1048608 | tf_op jit(solution)/shard_map/ppermute | solution.py:208
  851.5 4.5 fusion.25
  860.0 126.2 %while.31 = (s32[]{:T(128)}, f32[3072,256]{0,1:T(8,128)}, f32[3072,256]{0,1:T(8,128)}, bf16[4,512,256]{2,1,0:T(8,128)(2,1)}, s32[4]{0:T(128)S(1)}, /*index=5*/bf...) while((s32[]{:T(128)}, f32[3072,256]{0,1:T(8,128)}, ...), condition=%wide.region_15.16_spmd, body=%wide.region_13.15_spmd.sunk | while | flops 2045377024 | bytes 149492144 | solution.py:274
  870.7 4.3 multiply_reduce_fusion.5
  887.7 4.0 constant_dynamic-update-slice_fusion.16
  902.2 4.3 multiply_reduce_fusion.5
  919.2 4.0 constant_dynamic-update-slice_fusion.16
  933.7 4.3 multiply_reduce_fusion.5
  950.6 4.1 constant_dynamic-update-slice_fusion.16
  965.2 4.3 multiply_reduce_fusion.5
  982.2 4.0 constant_dynamic-update-slice_fusion.16
  998.0 4.6 add_add_fusion
  1002.7 10.1 fusion.82
  1013.5 12.6 fusion.68
  1026.2 4.9 fusion.17
  1031.2 4.5 fusion.81
  1039.2 4.3 fusion.61
  1043.8 4.8 fusion.42
  1052.8 106.4 %reduce-scatter.17.cloned.1.call-done = f32[512,1024]{1,0:T(8,128)} async-done(((f32[2048,1024]{1,0:T(8,128)}), f32[512,1024]{1,0:T(8,128)}) %reduce-scatter.17.cloned.1.call-update) | async-done | bytes 2097168 | tf_op jit(solution)/shard_map/reduce_scatter | solution.py:298
  1162.6 3.7 convert_reduce_fusion.1
  1166.3 42.2 %all-reduce.1 = (f32[1024]{0:T(1024)}, f32[512]{0:T(512)}, f32[1024]{0:T(1024)}, f32[1024]{0:T(1024)}, f32[1024]{0:T(1024)}, /*index=5*/f32[1024]{0:T(1024)}, f32[1024]{0:T(1024)}, f32[4096]{0:T(1024)}, f32[1024]{0:T(1024)}) all-reduce(f32[1024]{0:T(1024)S(1)} %dynamic_update_slice.42, ...), channel_id=1, replica_groups=mesh['seq'=8,'tp'=4] {'seq','tp'}, use_global_device_ids=true, to_apply=%region_20.21 | all-reduce | flops 11776 | bytes 94208 | tf_op jit(solution)/shard_map/psum | solution.py:313
  1208.6 6.4 reduce-scatter.27.cloned.1.call-done
  1215.0 55.0 %reduce-scatter.29.cloned.1.call-done = f32[1024,128]{1,0:T(8,128)} async-done(((f32[1024,1024]{1,0:T(8,128)}), f32[1024,128]{1,0:T(8,128)}) %reduce-scatter.29.cloned.1.call-update) | async-done | bytes 524304 | tf_op jit(solution)/shard_map/reduce_scatter | solution.py:333
  1270.0 39.6 %reduce-scatter.25.cloned.1.call-done = f32[256,128]{1,0:T(8,128)} async-done(((f32[256,1024]{1,0:T(8,128)}), f32[256,128]{1,0:T(8,128)}) %reduce-scatter.25.cloned.1.call-update) | async-done | bytes 131088 | tf_op jit(solution)/shard_map/reduce_scatter | solution.py:331
  1309.6 39.7 %reduce-scatter.19.cloned.1.call-done = f32[128,256]{1,0:T(8,128)} async-done(((f32[1024,256]{1,0:T(8,128)}), f32[128,256]{1,0:T(8,128)}) %reduce-scatter.19.cloned.1.call-update) | async-done | bytes 131088 | tf_op jit(solution)/shard_map/reduce_scatter | solution.py:328
  1349.3 37.7 %reduce-scatter.23.cloned.1.call-done = f32[128,128]{1,0:T(8,128)} async-done(((f32[1024,128]{1,0:T(8,128)}), f32[128,128]{1,0:T(8,128)}) %reduce-scatter.23.cloned.1.call-update) | async-done | bytes 65552 | tf_op jit(solution)/shard_map/reduce_scatter | solution.py:330
  1387.0 39.7 %reduce-scatter.21.cloned.1.call-done = f32[128,256]{1,0:T(8,128)} async-done(((f32[1024,256]{1,0:T(8,128)}), f32[128,256]{1,0:T(8,128)}) %reduce-scatter.21.cloned.1.call-update) | async-done | bytes 131088 | tf_op jit(solution)/shard_map/reduce_scatter | solution.py:329
  (327 shorter events, 219.9 us)
Async XLA Ops:
  7.2 428.7 %copy-start = (bf16[1024,1024]{1,0:T(8,128)(2,1)S(1)}, bf16[1024,1024]{1,0:T(8,128)(2,1)}, u32[]{:S(2)}) copy-start(bf16[1024,1024]{1,0:T(8,128)(2,1)} %param.37) | copy-start | bytes 6291460
  7.2 6.1 copy-start.26
  7.2 89.7 %copy-start.20 = (bf16[1024,128]{1,0:T(8,128)(2,1)S(1)}, bf16[1024,128]{1,0:T(8,128)(2,1)}, u32[]{:S(2)}) copy-start(bf16[1024,128]{1,0:T(8,128)(2,1)} %param.31) | copy-start | bytes 786436
  7.2 89.6 %copy-start.43 = (f32[128]{0:T(128)S(1)}, f32[128]{0:T(128)}, u32[]{:S(2)}) copy-start(f32[128]{0:T(128)} %param.32) | copy-start | bytes 1540
  7.2 89.6 %all-gather.4.cloned.1.call-start = ((), (), s32[]{:S(2)}) async-start(), calls=%async_computation.10 | async-start | bytes 5242880 | tf_op jit(solution)/shard_map/all_gather | solution.py:114
  8.9 4.4 copy-start.27
  13.3 336.5 %reduce-scatter.11.cloned.1.call-start = ((), (), s32[]{:S(2)}) async-start(), calls=%async_computation.11 | async-start | bytes 10485760 | tf_op jit(solution)/shard_map/reduce_scatter | solution.py:165
  103.5 4.7 copy-start.18
  103.5 8.6 copy-start.30
  103.5 8.6 copy-start.47
  109.2 10.8 collective-permute-start
  122.0 5.9 copy-start.13
  130.3 64.8 %copy-start.22 = (bf16[256,1024]{1,0:T(8,128)(2,1)S(1)}, bf16[256,1024]{1,0:T(8,128)(2,1)}, u32[]{:S(2)}) copy-start(bf16[256,1024]{1,0:T(8,128)(2,1)} %param.33) | copy-start | bytes 1572868
  200.8 148.9 %copy-start.7 = (bf16[512,1024]{1,0:T(8,128)(2,1)S(1)}, bf16[512,1024]{1,0:T(8,128)(2,1)}, u32[]{:S(2)}) copy-start(bf16[512,1024]{1,0:T(8,128)(2,1)} %param.23) | copy-start | bytes 3145732
  200.8 148.9 %copy-start.42 = (f32[1024]{0:T(1024)S(1)}, f32[1024]{0:T(1024)}, u32[]{:S(2)}) copy-start(f32[1024]{0:T(1024)} %param.34) | copy-start | bytes 12292
  200.8 152.2 %copy-start.31 = (f32[1024]{0:T(1024)S(1)}, f32[1024]{0:T(1024)}, u32[]{:S(2)}) copy-start(f32[1024]{0:T(1024)} %param.35) | copy-start | bytes 12292
  200.8 152.2 %copy-start.40 = (f32[1024]{0:T(1024)S(1)}, f32[1024]{0:T(1024)}, u32[]{:S(2)}) copy-start(f32[1024]{0:T(1024)} %param.36) | copy-start | bytes 12292
  200.8 235.1 %all-gather.6.cloned.1.call-start = ((), (), s32[]{:S(2)}) async-start(), calls=%async_computation.12 | async-start | bytes 5242880 | tf_op jit(solution)/shard_map/all_gather | solution.py:174
  354.4 162.2 %all-gather.8.cloned.1.call-start = ((), (), s32[]{:S(2)}) async-start(), calls=%async_computation.14 | async-start | bytes 5242880 | tf_op jit(solution)/shard_map/all_gather | solution.py:191
  355.0 161.6 %copy-start.45 = (f32[1024]{0:T(1024)S(1)}, f32[1024]{0:T(1024)}, u32[]{:S(2)}) copy-start(f32[1024]{0:T(1024)} %param.38) | copy-start | bytes 12292
  355.0 326.5 %reduce-scatter.15.cloned.1.call-start = ((), (), s32[]{:S(2)}) async-start(), calls=%async_computation.15 | async-start | bytes 10485760 | tf_op jit(solution)/shard_map/reduce_scatter | solution.py:198
  538.3 222.9 %reduce-scatter.13.cloned.1.call-start = ((), (), s32[]{:S(2)}) async-start(), calls=%async_computation.13 | async-start | bytes 5242880 | tf_op jit(solution)/shard_map/reduce_scatter | solution.py:180
  551.3 130.2 %copy-start.6 = (f32[512,1024]{1,0:T(8,128)S(1)}, f32[512,1024]{1,0:T(8,128)}, u32[]{:S(2)}) copy-start(f32[512,1024]{1,0:T(8,128)} %copy-done.5) | copy-start | bytes 6291460
  551.3 209.8 %copy-start.41 = (f32[1024]{0:T(1024)S(1)}, f32[1024]{0:T(1024)}, u32[]{:S(2)}) copy-start(f32[1024]{0:T(1024)} %param.40) | copy-start | bytes 12292
  551.3 607.9 %reduce-scatter.17.cloned.1.call-start = ((), (), s32[]{:S(2)}) async-start(), calls=%async_computation.16 | async-start | bytes 10485760 | tf_op jit(solution)/shard_map/reduce_scatter | solution.py:298
  684.5 81.7 %copy-start.11 = (bf16[512,1024]{1,0:T(8,128)(2,1)S(1)}, bf16[512,1024]{1,0:T(8,128)(2,1)}, u32[]{:S(2)}) copy-start(bf16[512,1024]{1,0:T(8,128)(2,1)} %param.41) | copy-start | bytes 3145732
  764.8 60.2 %copy-start.34 = (f32[512]{0:T(512)}, f32[512]{0:T(512)S(1)}, u32[]{:S(2)}) copy-start(f32[512]{0:T(512)S(1)} %negate_multiply_fusion.1) | copy-start | bytes 6148
  767.4 25.2 %collective-permute-start.1 = (bf16[512,1024]{1,0:T(8,128)(2,1)S(1)}, bf16[512,1024]{1,0:T(8,128)(2,1)S(1)}, u32[]{:S(2)}, u32[]{:S(2)}) collective-permute-start(bf16[512,1024]{1,0:T(8,128)(2,1)S(1)} %get-tuple-element.377), channel_id=1, source_target_pairs={{0,3},{1,0},{2,1},{3,2},{4,7},{5,4},{6,5},{7,6},{8,11},{9,8},{10,9... | collective-permute-start | bytes 3145736 | tf_op jit(solution)/shard_map/ppermute | solution.py:208
  792.6 26.0 %collective-permute-start.2 = (bf16[512,1024]{1,0:T(8,128)(2,1)S(1)}, bf16[512,1024]{1,0:T(8,128)(2,1)S(1)}, u32[]{:S(2)}, u32[]{:S(2)}) collective-permute-start(bf16[512,1024]{1,0:T(8,128)(2,1)S(1)} %collective-permute-done.1), channel_id=1, source_target_pairs={{0,3},{1,0},{2,1},{3,2},{4,7},{5,4},{6,5},{7,6},{8,11},{9,8},{10,9... | collective-permute-start | bytes 3145736 | tf_op jit(solution)/shard_map/ppermute | solution.py:208
  818.6 25.1 %collective-permute-start.3 = (bf16[512,1024]{1,0:T(8,128)(2,1)S(1)}, bf16[512,1024]{1,0:T(8,128)(2,1)}, u32[]{:S(2)}, u32[]{:S(2)}) collective-permute-start(bf16[512,1024]{1,0:T(8,128)(2,1)S(1)} %collective-permute-done.2), channel_id=1, source_target_pairs={{0,3},{1,0},{2,1},{3,2},{4,7},{5,4},{6,5},{7,6},{8,11},{9,8},{10,9... | collective-permute-start | bytes 3145736 | tf_op jit(solution)/shard_map/ppermute | solution.py:208
  846.0 5.5 copy-start.23
  987.5 4.0 copy-start.12
  987.6 4.0 copy-start.24
  989.9 8.1 copy-start.17
  990.0 4.6 collective-permute-start.4
  1002.7 212.3 %reduce-scatter.27.cloned.1.call-start = ((), (), s32[]{:S(2)}) async-start(), calls=%async_computation.21 | async-start | bytes 4718592 | tf_op jit(solution)/shard_map/reduce_scatter | solution.py:332
  1012.9 257.1 %reduce-scatter.29.cloned.1.call-start = ((), (), s32[]{:S(2)}) async-start(), calls=%async_computation.22 | async-start | bytes 4718592 | tf_op jit(solution)/shard_map/reduce_scatter | solution.py:333
  1026.2 283.4 %reduce-scatter.25.cloned.1.call-start = ((), (), s32[]{:S(2)}) async-start(), calls=%async_computation.20 | async-start | bytes 1179648 | tf_op jit(solution)/shard_map/reduce_scatter | solution.py:331
  1031.1 318.2 %reduce-scatter.19.cloned.1.call-start = ((), (), s32[]{:S(2)}) async-start(), calls=%async_computation.17 | async-start | bytes 1179648 | tf_op jit(solution)/shard_map/reduce_scatter | solution.py:328
  1035.6 351.3 %reduce-scatter.23.cloned.1.call-start = ((), (), s32[]{:S(2)}) async-start(), calls=%async_computation.19 | async-start | bytes 589824 | tf_op jit(solution)/shard_map/reduce_scatter | solution.py:330
  1043.5 383.2 %reduce-scatter.21.cloned.1.call-start = ((), (), s32[]{:S(2)}) async-start(), calls=%async_computation.18 | async-start | bytes 1179648 | tf_op jit(solution)/shard_map/reduce_scatter | solution.py:329
  1048.6 110.6 %copy-start.8 = (bf16[512,1024]{1,0:T(8,128)(2,1)S(1)}, bf16[512,1024]{1,0:T(8,128)(2,1)}, u32[]{:S(2)}) copy-start(bf16[512,1024]{1,0:T(8,128)(2,1)} %param.23) | copy-start | bytes 3145732
  1048.6 110.6 %copy-start.28 = (f32[512]{0:T(512)S(1)}, f32[512]{0:T(512)}, u32[]{:S(2)}) copy-start(f32[512]{0:T(512)} %copy-done.27) | copy-start | bytes 6148
  1048.6 110.6 %copy-start.29 = (f32[1024]{0:T(1024)S(1)}, f32[1024]{0:T(1024)}, u32[]{:S(2)}) copy-start(f32[1024]{0:T(1024)} %param.26) | copy-start | bytes 12292
  1049.7 111.7 %copy-start.37 = (f32[512]{0:T(512)S(1)}, f32[512]{0:T(512)}, u32[]{:S(2)}) copy-start(f32[512]{0:T(512)} %copy-done.36) | copy-start | bytes 6148
  1049.7 111.7 %copy-start.33 = (f32[512]{0:T(512)S(1)}, f32[512]{0:T(512)}, u32[]{:S(2)}) copy-start(f32[512]{0:T(512)} %copy-done.32) | copy-start | bytes 6148
  1050.0 112.5 %copy-start.35 = (f32[512]{0:T(512)S(1)}, f32[512]{0:T(512)}, u32[]{:S(2)}) copy-start(f32[512]{0:T(512)} %copy-done.34) | copy-start | bytes 6148
  1162.5 264.1 %copy-start.1 = (bf16[1024,1024]{1,0:T(8,128)(2,1)S(1)}, bf16[1024,1024]{1,0:T(8,128)(2,1)}, u32[]{:S(2)}) copy-start(bf16[1024,1024]{1,0:T(8,128)(2,1)} %param.37) | copy-start | bytes 6291460
  (24 other events, 58.5 us)
Sparse Core Ops, SparseCore 0:
  13.4 83.4 all-gather.3
  200.9 148.7 reduce-scatter.10
  354.5 81.3 all-gather.5
  437.3 79.2 all-gather.7
  538.4 143.0 reduce-scatter.14
  683.7 77.4 reduce-scatter.12
  1002.8 156.3 reduce-scatter.16
  1163.1 51.8 reduce-scatter.26
  1218.9 51.0 reduce-scatter.28
  1273.6 35.9 reduce-scatter.24
  1313.3 35.9 reduce-scatter.18
  1352.8 34.1 reduce-scatter.22
  1390.7 35.9 reduce-scatter.20
